TPU v7x, 32 devices: a whole 2x2x4 slice. The times are simulated.
32 devices in a mesh: grp: 2 (over y), seq: 4 (over z), head: 2 (over x), clip: 2 (over core).
Axes of the slice: x: 2, y: 2, z: 4, core: 2. Of those that a mesh axis runs over, the one named last changes fastest.
Arguments:
- query_states: bfloat16 [4, 2048, 1536], P(('grp', 'clip'), 'seq', 'head'), parts along dimension 0, may hold values from -64 to 64
- key_states: bfloat16 [4, 2048, 1536], P(('grp', 'clip'), 'seq', 'head'), parts along dimension 0, may hold values from -4 to 4
- value_states: bfloat16 [4, 2048, 1536], P(('grp', 'clip'), 'seq', 'head'), parts along dimension 0, may hold values from -5 to 5
- output_grad: bfloat16 [4, 2048, 3072], P(('grp', 'clip'), 'seq', 'head'), parts along dimension 0, may hold values from -48 to 48
- w_out: bfloat16 [1536, 3072], P('head'), may hold values from -0.15625 to 0.15625
- key_list: int32 [4, 8, 8], P(('grp', 'clip')), parts along dimension 0, may hold values from 0 to 7, as said below
- key_count: int32 [4, 8], P(('grp', 'clip')), parts along dimension 0, may hold values from 1 to 8, as said below
Outputs:
- query_grad: bfloat16 [4, 2048, 1536], P(('grp', 'clip'), 'seq', 'head'), parts along dimension 0
- key_grad: bfloat16 [4, 2048, 1536], P(('grp', 'clip'), 'seq', 'head'), parts along dimension 0
- value_grad: bfloat16 [4, 2048, 1536], P(('grp', 'clip'), 'seq', 'head'), parts along dimension 0
- grad_features: float32 [4, 12, 3], P(('grp', 'clip'), 'head'), parts along dimension 0
There are 2 independent parts, one for each index of `grp`. A program takes and returns all parts, laid end to end along the dimension named above; an argument that names none is the same for every part. Nothing has to cross between parts.
Inputs may be any that keep to these rules, and one draw needn't show every extreme that they name: Tile i lies in frame block i // 4 at place i % 4. For each clip and query tile i the first key_count entries of key_list are distinct key tiles in ascending order, among them i itself, each at a place within 2 of i's place, in i's frame block or in the other one; the remaining entries equal i. `key_count`: in every draw some query tile lists 8 key tiles.
All inputs are finite; a program needn't handle non-finite values.
Results may differ from a plain program's by a relative error of at most 0.035.
Values may be sent and summed in bfloat16 or wider, within the bound.
No kernel may reach another device: no remote copies, remote signals or barrier semaphores. Data moves between devices by JAX's collectives and lax.ppermute only.
A program may use at most 128 MiB of HBM per device.

v0:
```python
import jax
import jax.numpy as jnp
from jax import lax
from jax.sharding import PartitionSpec as P

HD = 128
TILE = 256


def attend(query_tiles, key_buf, value_buf, grad_tiles, buf_slots, counts):
    score_scale = HD ** (-0.5)
    tile_count, tile_rows, feat_width = query_tiles.shape
    slot_count = buf_slots.shape[1]
    key_span = slot_count * tile_rows
    buf_tiles = key_buf.shape[0]
    key_sel = key_buf[buf_slots].reshape(tile_count, key_span, feat_width)
    value_sel = value_buf[buf_slots].reshape(tile_count, key_span, feat_width)
    allowed = jnp.arange(key_span)[None, :] // tile_rows < counts[:, None]

    def head_step(head_idx, carried):
        query_acc, key_acc, value_acc = carried
        col_start = head_idx * HD
        query_head = lax.dynamic_slice_in_dim(query_tiles, col_start, HD, 2)
        key_head = lax.dynamic_slice_in_dim(key_sel, col_start, HD, 2)
        value_head = lax.dynamic_slice_in_dim(value_sel, col_start, HD, 2)
        grad_head = lax.dynamic_slice_in_dim(grad_tiles, col_start, HD, 2)
        scores = (
            jnp.einsum("iqe,ike->iqk", query_head, key_head, preferred_element_type=jnp.float32)
            * score_scale
        )
        scores = jnp.where(allowed[:, None, :], scores, -jnp.inf)
        row_max = jnp.max(scores, axis=-1, keepdims=True)
        log_norm = row_max + jnp.log(jnp.sum(jnp.exp(scores - row_max), axis=-1, keepdims=True))
        weights = jnp.exp(scores - log_norm)
        weights_b = weights.astype(jnp.bfloat16)
        attn_out = jnp.einsum(
            "iqk,ike->iqe", weights_b, value_head, preferred_element_type=jnp.float32
        ).astype(jnp.bfloat16)
        row_delta = jnp.sum(
            grad_head.astype(jnp.float32) * attn_out.astype(jnp.float32), axis=-1, keepdims=True
        )
        dprob = jnp.einsum(
            "iqe,ike->iqk", grad_head, value_head, preferred_element_type=jnp.float32
        )
        dscore = (weights * (dprob - row_delta)).astype(jnp.bfloat16)
        query_head_grad = score_scale * jnp.einsum(
            "iqk,ike->iqe", dscore, key_head, preferred_element_type=jnp.float32
        )
        key_head_grad = score_scale * jnp.einsum(
            "iqk,iqe->ike", dscore, query_head, preferred_element_type=jnp.float32
        )
        value_head_grad = jnp.einsum(
            "iqk,iqe->ike", weights_b, grad_head, preferred_element_type=jnp.float32
        )
        query_acc = lax.dynamic_update_slice_in_dim(query_acc, query_head_grad, col_start, 2)
        key_acc = lax.dynamic_update_slice_in_dim(key_acc, key_head_grad, col_start, 2)
        value_acc = lax.dynamic_update_slice_in_dim(value_acc, value_head_grad, col_start, 2)
        return (query_acc, key_acc, value_acc)

    start_state = (
        jnp.zeros((tile_count, tile_rows, feat_width), jnp.float32),
        jnp.zeros((tile_count, key_span, feat_width), jnp.float32),
        jnp.zeros((tile_count, key_span, feat_width), jnp.float32),
    )
    query_full, key_sel_grad, value_sel_grad = lax.fori_loop(
        0, feat_width // HD, head_step, start_state
    )
    live_slot = jnp.arange(slot_count)[None, :] < counts[:, None]
    routing = (
        (buf_slots[:, :, None] == jnp.arange(buf_tiles)[None, None, :]) & live_slot[:, :, None]
    ).astype(jnp.float32)
    key_grad_buf = jnp.einsum(
        "imb,imr->br",
        routing,
        key_sel_grad.reshape(tile_count, slot_count, tile_rows * feat_width),
        precision=lax.Precision.HIGHEST,
    )
    value_grad_buf = jnp.einsum(
        "imb,imr->br",
        routing,
        value_sel_grad.reshape(tile_count, slot_count, tile_rows * feat_width),
        precision=lax.Precision.HIGHEST,
    )
    return (
        query_full,
        key_grad_buf.reshape(buf_tiles, tile_rows, feat_width),
        value_grad_buf.reshape(buf_tiles, tile_rows, feat_width),
    )


def head_squares(grads_full, head_count):
    rows = grads_full.reshape(-1, head_count, HD)
    return jnp.sum(rows * rows, axis=(0, 2))


def per_device(query_states, key_states, value_states, output_grad, w_out, key_list, key_count):
    seq_count = lax.axis_size("seq")
    seq_index = lax.axis_index("seq")
    tok_rows = query_states.shape[1]
    feat_width = query_states.shape[2]
    head_count = feat_width // HD
    tile_count = tok_rows // TILE
    first_tile = seq_index * tile_count
    own_lists = lax.dynamic_slice_in_dim(key_list[0], first_tile, tile_count, 0)
    own_counts = lax.dynamic_slice_in_dim(key_count[0], first_tile, tile_count, 0)
    grad_out = lax.dot_general(
        lax.all_gather(output_grad, "head", axis=2, tiled=True)[0],
        w_out,
        (((1,), (1,)), ((), ())),
        preferred_element_type=jnp.float32,
    ).astype(jnp.bfloat16)
    query_tiles = query_states[0].reshape(tile_count, TILE, feat_width)
    grad_tiles = grad_out.reshape(tile_count, TILE, feat_width)
    key_whole, value_whole = (
        lax.all_gather(key_states, "seq", axis=1, tiled=True),
        lax.all_gather(value_states, "seq", axis=1, tiled=True),
    )
    key_buf = key_whole[0].reshape(-1, TILE, feat_width)
    value_buf = value_whole[0].reshape(-1, TILE, feat_width)
    query_full, key_grad_buf, value_grad_buf = attend(
        query_tiles, key_buf, value_buf, grad_tiles, own_lists, own_counts
    )
    buf_rows = key_grad_buf.shape[0] * TILE
    key_sum, value_sum = (
        lax.psum_scatter(
            key_grad_buf.reshape(1, buf_rows, feat_width).astype(jnp.bfloat16),
            "seq",
            scatter_dimension=1,
            tiled=True,
        ).astype(jnp.float32),
        lax.psum_scatter(
            value_grad_buf.reshape(1, buf_rows, feat_width).astype(jnp.bfloat16),
            "seq",
            scatter_dimension=1,
            tiled=True,
        ).astype(jnp.float32),
    )
    key_full = key_sum[0]
    value_full = value_sum[0]
    query_rows = query_full.reshape(tok_rows, feat_width)
    local_sums = jnp.stack(
        [
            head_squares(query_rows, head_count),
            head_squares(key_full, head_count),
            head_squares(value_full, head_count),
        ],
        axis=-1,
    )
    total_sums = lax.psum(local_sums, "seq")
    grad_features = jnp.log(total_sums / (seq_count * tok_rows * HD) + 1e-06)
    return (
        query_rows.astype(jnp.bfloat16)[None],
        key_full.astype(jnp.bfloat16)[None],
        value_full.astype(jnp.bfloat16)[None],
        grad_features[None],
    )


def solution(mesh):
    in_specs = (
        P(("grp", "clip"), "seq", "head"),
        P(("grp", "clip"), "seq", "head"),
        P(("grp", "clip"), "seq", "head"),
        P(("grp", "clip"), "seq", "head"),
        P("head", None),
        P(("grp", "clip"), None, None),
        P(("grp", "clip"), None),
    )
    out_specs = (
        P(("grp", "clip"), "seq", "head"),
        P(("grp", "clip"), "seq", "head"),
        P(("grp", "clip"), "seq", "head"),
        P(("grp", "clip"), "head", None),
    )
    return jax.shard_map(
        per_device, mesh=mesh, in_specs=in_specs, out_specs=out_specs, check_vma=False
    )
```

profile of v0, /device:TPU:0, one launch (start us, length us, event | category | flops | bytes accessed | tf_op | source)
XLA Modules:
  0.0 461.2 jit_solution(8411246772068753391)
XLA Ops:
  11.1 46.2 %all-gather.6.cloned.1.call-done = bf16[1,512,3072]{2,1,0:T(8,128)(2,1)} async-done(((bf16[1,512,1536]{2,1,0:T(8,128)(2,1)}), bf16[1,512,3072]{2,1,0:T(8,128)(2,1)}) %all-gather.6.cloned.1.call-update) | async-done | bytes 3145744 | tf_op jit(solution)/shard_map/all_gather | solution.py:107
  57.3 5.9 %fusion.28 = bf16[512,768]{1,0:T(8,128)(2,1)S(1)} fusion(bf16[768,3072]{1,0:T(8,128)(2,1)} %param.13, bf16[1,512,3072]{2,1,0:T(8,128)(2,1)} %all-gather.6.cloned.1.call-done), kind=kOutput, calls=%fused_computation.42 | convolution fusion | flops 2416312320 | bytes 8650752 | tf_op jit(solution)/shard_map/dot_general | solution.py:106
  63.2 59.1 %all-gather.4.cloned.1.call-done = bf16[1,2048,768]{2,1,0:T(8,128)(2,1)} async-done(((bf16[1,512,768]{2,1,0:T(8,128)(2,1)}), bf16[1,2048,768]{2,1,0:T(8,128)(2,1)}) %all-gather.4.cloned.1.call-update) | async-done | bytes 3145744 | tf_op jit(solution)/shard_map/all_gather | solution.py:115
  122.3 5.6 %gather_fusion = bf16[16,256,768]{2,1,0:T(8,128)(2,1)} fusion(bf16[8,256,768]{2,1,0:T(8,128)(2,1)} %bitcast.50, s32[1024]{0:T(1024)S(1)} %pad_clamp_fusion), kind=kCustom, calls=%fused_computation | custom fusion | bytes 12582976 | tf_op jit(solution)/shard_map/gather | solution.py:16
  127.9 58.1 %all-gather.8.cloned.1.call-done = bf16[1,2048,768]{2,1,0:T(8,128)(2,1)} async-done(((bf16[1,512,768]{2,1,0:T(8,128)(2,1)}), bf16[1,2048,768]{2,1,0:T(8,128)(2,1)}) %all-gather.8.cloned.1.call-update) | async-done | bytes 3145744 | tf_op jit(solution)/shard_map/all_gather | solution.py:116
  186.0 5.5 %gather_fusion.1 = bf16[16,256,768]{2,1,0:T(8,128)(2,1)} fusion(bf16[8,256,768]{2,1,0:T(8,128)(2,1)} %bitcast.51, s32[1024]{0:T(1024)S(1)} %pad_clamp_fusion), kind=kCustom, calls=%fused_computation.1 | custom fusion | bytes 12582976 | tf_op jit(solution)/shard_map/gather | solution.py:17
  191.5 5.4 %broadcast.103 = f32[2,2048,768]{2,1,0:T(8,128)} broadcast(f32[]{:T(128)} %constant.78.clone.1), dimensions={} | broadcast | bytes 12582916 | tf_op jit(solution)/shard_map/broadcast.13
  196.9 5.3 %broadcast.103.clone = f32[2,2048,768]{2,1,0:T(8,128)} broadcast(f32[]{:T(128)} %constant.78.clone.1), dimensions={} | broadcast | bytes 12582916 | tf_op jit(solution)/shard_map/broadcast.13
  202.3 92.5 %while.18 = (s32[]{:T(128)}, f32[2,256,768]{2,1,0:T(8,128)S(1)}, f32[2,2048,768]{2,1,0:T(8,128)}, f32[2,2048,768]{2,1,0:T(8,128)}, bf16[2,256,768]{2,1,0:T(8,128...) while((s32[]{:T(128)}, f32[2,256,768]{2,1,0:T(8,128)S(1)}, ...), condition=%wide.region_4.5_spmd.clone, body=%wide.region_0.4_spmd.clone.sunk | while | flops 1625164800 | bytes 36614328 | solution.py:65
  202.6 2.1 fusion.71
  204.7 0.7 exponential_reduce_fusion.2
  205.4 2.6 convolution_dynamic-update-slice_fusion.2
  208.0 2.2 fusion.72
  210.2 2.3 multiply_convert_fusion.2
  212.5 3.4 fusion.74
  215.9 1.9 fusion.73
  217.9 2.1 fusion.71
  220.0 0.7 exponential_reduce_fusion.2
  220.8 2.6 convolution_dynamic-update-slice_fusion.2
  223.4 2.2 fusion.72
  225.6 2.3 multiply_convert_fusion.2
  227.9 3.3 fusion.74
  231.2 1.9 fusion.73
  233.3 2.1 fusion.71
  235.4 0.7 exponential_reduce_fusion.2
  236.1 2.7 convolution_dynamic-update-slice_fusion.2
  238.8 2.2 fusion.72
  240.9 2.3 multiply_convert_fusion.2
  243.2 3.3 fusion.74
  246.6 1.9 fusion.73
  248.6 2.1 fusion.71
  250.7 0.7 exponential_reduce_fusion.2
  251.5 2.8 convolution_dynamic-update-slice_fusion.2
  254.2 2.2 fusion.72
  256.4 2.3 multiply_convert_fusion.2
  258.7 3.4 fusion.74
  262.1 1.9 fusion.73
  264.1 2.1 fusion.71
  267.0 2.7 convolution_dynamic-update-slice_fusion.2
  269.7 2.2 fusion.72
  271.8 2.3 multiply_convert_fusion.2
  274.1 3.4 fusion.74
  277.5 1.9 fusion.73
  279.6 2.1 fusion.71
  281.7 0.7 exponential_reduce_fusion.2
  282.4 2.6 convolution_dynamic-update-slice_fusion.2
  285.0 2.2 fusion.72
  287.2 2.3 multiply_convert_fusion.2
  289.5 3.4 fusion.74
  292.8 1.9 fusion.73
  294.8 1.1 copy-done.2
  295.9 13.2 %reshape.176 = f32[2,8,196608]{2,1,0:T(8,128)} reshape(f32[2,2048,768]{2,1,0:T(8,128)} %get-tuple-element.161) | data formatting | bytes 25165824 | tf_op jit(solution)/shard_map/reshape | solution.py:75
  309.2 7.6 %fusion.24 = bf16[8,196608]{1,0:T(8,128)(2,1)S(1)} fusion(f32[2,8,196608]{2,1,0:T(8,128)} %reshape.176, s32[2,8]{1,0:T(2,128)S(1)} %dynamic-slice_bitcast_fusion, pred[2,8]{1,0:T(4,128)(4,1)S(1)} %iota_compare_fusion.1), kind=kOutput, calls=%fused_computation.35 | convolution fusion | flops 303563008 | bytes 15728720 | tf_op jit(solution)/shard_map/imb,imr->br/dot_general | solution.py:72
  316.8 3.2 convert_element_type.94
  320.0 13.3 %reshape.177 = f32[2,8,196608]{2,1,0:T(8,128)} reshape(f32[2,2048,768]{2,1,0:T(8,128)} %get-tuple-element.162) | data formatting | bytes 25165824 | tf_op jit(solution)/shard_map/reshape | solution.py:81
  333.3 7.6 %fusion.25 = bf16[8,196608]{1,0:T(8,128)(2,1)S(1)} fusion(f32[2,8,196608]{2,1,0:T(8,128)} %reshape.177, s32[2,8]{1,0:T(2,128)S(1)} %dynamic-slice_bitcast_fusion, pred[2,8]{1,0:T(4,128)(4,1)S(1)} %iota_compare_fusion.1), kind=kOutput, calls=%fused_computation.36 | convolution fusion | flops 303563008 | bytes 15728720 | tf_op jit(solution)/shard_map/imb,imr->br/dot_general | solution.py:78
  341.0 3.1 convert_element_type.96
  344.1 1.4 copy-done.3
  345.5 1.0 multiply_reduce_fusion.2
  346.6 32.6 %reduce-scatter.3.cloned.1.call-done = bf16[1,512,768]{2,1,0:T(8,128)(2,1)} async-done(((bf16[1,2048,768]{2,1,0:T(8,128)(2,1)}), bf16[1,512,768]{2,1,0:T(8,128)(2,1)}) %reduce-scatter.3.cloned.1.call-update) | async-done | bytes 786448 | tf_op jit(solution)/shard_map/reduce_scatter | solution.py:125
  379.2 1.3 multiply_reduce_fusion.1
  380.6 61.6 %reduce-scatter.5.cloned.1.call-done = bf16[1,512,768]{2,1,0:T(8,128)(2,1)} async-done(((bf16[1,2048,768]{2,1,0:T(8,128)(2,1)}), bf16[1,512,768]{2,1,0:T(8,128)(2,1)}) %reduce-scatter.5.cloned.1.call-update) | async-done | bytes 786448 | tf_op jit(solution)/shard_map/reduce_scatter | solution.py:131
  442.2 1.3 multiply_reduce_fusion
  443.7 10.4 %psum.7 = f32[6,3]{0,1:T(4,128)S(1)} all-reduce(f32[6,3]{0,1:T(4,128)S(1)} %pad_maximum_fusion), channel_id=1, replica_groups=mesh['grp'=2,'seq'=4,'head'=2,'clip'=2] {'seq'}, use_global_device_ids=true, to_apply=%region_13.14 | all-reduce | flops 18 | bytes 144 | tf_op jit(solution)/shard_map/psum | solution.py:149
  (43 shorter events, 6.2 us)
Async XLA Ops:
  7.2 3.1 copy-start
  7.2 50.1 %all-gather.6.cloned.1.call-start = ((), (), s32[]{:S(2)}) async-start(), calls=%async_computation.3 | async-start | bytes 4718592 | tf_op jit(solution)/shard_map/all_gather | solution.py:107
  7.9 114.4 %all-gather.4.cloned.1.call-start = ((), (), s32[]{:S(2)}) async-start(), calls=%async_computation.2 | async-start | bytes 3932160 | tf_op jit(solution)/shard_map/all_gather | solution.py:115
  8.7 177.3 %all-gather.8.cloned.1.call-start = ((), (), s32[]{:S(2)}) async-start(), calls=%async_computation.4 | async-start | bytes 3932160 | tf_op jit(solution)/shard_map/all_gather | solution.py:116
  9.4 369.8 %reduce-scatter.3.cloned.1.call-start = ((), (), s32[]{:S(2)}) async-start(), calls=%async_computation.5 | async-start | bytes 3932160 | tf_op jit(solution)/shard_map/reduce_scatter | solution.py:125
  294.8 1.1 copy-start.2
  320.0 122.3 %reduce-scatter.5.cloned.1.call-start = ((), (), s32[]{:S(2)}) async-start(), calls=%async_computation.6 | async-start | bytes 3932160 | tf_op jit(solution)/shard_map/reduce_scatter | solution.py:131
  340.9 113.7 %copy-start.1 = (s32[1,8]{1,0:T(1,128)S(1)}, s32[1,8]{1,0:T(1,128)}, u32[]{:S(2)}) copy-start(s32[1,8]{1,0:T(1,128)} %param.15) | copy-start | bytes 100
  344.0 1.4 copy-start.3
Sparse Core Ops, SparseCore 0:
  9.5 47.6 all-gather.5
  58.8 63.4 all-gather.3
  123.9 62.0 all-gather.7
  320.1 59.0 reduce-scatter.2
  381.9 60.3 reduce-scatter.4
where the time goes:
time: 463 us; the launch traced here: 461 us
  waiting for transfers between devices  260 us (56%)
  matrix products  108 us (23%)
  local copies, waits for them, and re-layouts  58.6 us (13%)
  between operations  13.9 us (3%)
  blocking collectives  10.4 us (2%)
  other arithmetic  9.63 us (2%)
    reduce_scatter x1, waiting for transfers between devices, per_device(): lax.psum_scatter(value_grad_buf.reshape(1, buf_rows, feat_width).astype(j...  61.6 us
    all_gather x1, waiting for transfers between devices, per_device(): lax.all_gather(key_states, 'seq', axis=1, tiled=True)  59.1 us
    all_gather x1, waiting for transfers between devices, per_device(): lax.all_gather(value_states, 'seq', axis=1, tiled=True)  58.1 us
    all_gather x1, waiting for transfers between devices, per_device(): lax.all_gather(output_grad, 'head', axis=2, tiled=True)[0]  46.2 us
    reduce_scatter x1, waiting for transfers between devices, per_device(): lax.psum_scatter(key_grad_buf.reshape(1, buf_rows, feat_width).astype(jnp...  32.6 us
    dot_general x6, matrix products, head_step(): jnp.einsum('iqk,iqe->ike', dscore, query_head, preferred_element_type=jnp...  20.2 us
    dot_general x6, matrix products, head_step(): jnp.einsum('iqk,iqe->ike', weights_b, grad_head, preferred_element_type=j...  16 us
    dot_general x6, matrix products, head_step(): jnp.einsum('iqe,ike->iqk', grad_head, value_head, preferred_element_type=...  13.7 us
  transfers between devices with their start and end apart: 5, of which 5 were waited for; matrix products, arithmetic and copies ran while one was open for 9% of the time, Pallas kernels for 0%

commit v1 on v0

--- a/solution.py
+++ b/solution.py
@@ -5,6 +5,27 @@
 
 HD = 128
 TILE = 256
+
+
+def collect(x, axis, dim):
+    peers, mine, width = (lax.axis_size(axis), lax.axis_index(axis), x.shape[dim])
+    ahead = [(i, (i + 1) % peers) for i in range(peers)]
+    behind = [(i, (i - 1) % peers) for i in range(peers)]
+    out = jnp.zeros((*x.shape[:dim], peers * width, *x.shape[dim + 1 :]), x.dtype)
+    out = lax.dynamic_update_slice_in_dim(out, x, mine * width, axis=dim)
+    from_left = from_right = x
+    halfway = peers // 2
+    for step in range(1, halfway + 1):
+        from_left = lax.ppermute(from_left, axis, ahead)
+        out = lax.dynamic_update_slice_in_dim(
+            out, from_left, (mine - step) % peers * width, axis=dim
+        )
+        if step < peers - halfway:
+            from_right = lax.ppermute(from_right, axis, behind)
+            out = lax.dynamic_update_slice_in_dim(
+                out, from_right, (mine + step) % peers * width, axis=dim
+            )
+    return out
 
 
 def attend(query_tiles, key_buf, value_buf, grad_tiles, buf_slots, counts):
@@ -113,7 +134,7 @@
     grad_tiles = grad_out.reshape(tile_count, TILE, feat_width)
     key_whole, value_whole = (
         lax.all_gather(key_states, "seq", axis=1, tiled=True),
-        lax.all_gather(value_states, "seq", axis=1, tiled=True),
+        collect(value_states, "seq", 1),
     )
     key_buf = key_whole[0].reshape(-1, TILE, feat_width)
     value_buf = value_whole[0].reshape(-1, TILE, feat_width)

time: 463 us -> 399 us (0.86)
  waiting for transfers between devices: 260 us -> 188 us
  starting transfers between devices: 0.19 us -> 5.36 us
    all_gather x1 -> x0, waiting for transfers between devices: 58.1 us -> none  [per_device(): lax.all_gather(value_states, 'seq', axis=1, tiled=True)]
    all_gather x1, waiting for transfers between devices: 46.2 us -> 0.01 us  [per_device(): lax.all_gather(output_grad, 'head', axis=2, tiled=True)[0]]
    ppermute x0 -> x3, waiting for transfers between devices: none -> 46.1 us  [the longest x2 33.2 us: collect(): from_left = lax.ppermute(from_left, axis, ahead)]
    all_gather x1, waiting for transfers between devices: 59.1 us -> 45.9 us  [per_device(): lax.all_gather(key_states, 'seq', axis=1, tiled=True)]
    ppermute x0 -> x3, starting transfers between devices: none -> 5.2 us  [the longest x2 3.11 us: collect(): from_left = lax.ppermute(from_left, axis, ahead)]
    dynamic_update_slice x0 -> x4, local copies, waits for them, and re-layouts: none -> 4.83 us  [the longest x2 2.45 us: collect(): lax.dynamic_update_slice_in_dim(out, from_left, (mine - step) % peers * w...]
  transfers between devices with their start and end apart: 5 -> 7, of which waited for: 5 -> 6; matrix products, arithmetic and copies ran while one was open for 9% -> 11% of each run, Pallas kernels for 0% -> 0%
where the time goes in v1:
time: 399 us; the launch traced here: 397 us
  waiting for transfers between devices  188 us (47%)
  matrix products  108 us (27%)
  local copies, waits for them, and re-layouts  61.8 us (15%)
  between operations  13.9 us (3%)
  blocking collectives  10.4 us (3%)
  other arithmetic  9.63 us (2%)
  starting transfers between devices  5.36 us (1%)
    reduce_scatter x1, waiting for transfers between devices, per_device(): lax.psum_scatter(value_grad_buf.reshape(1, buf_rows, feat_width).astype(j...  61.6 us
    all_gather x1, waiting for transfers between devices, per_device(): lax.all_gather(key_states, 'seq', axis=1, tiled=True)  45.9 us
    ppermute x2, waiting for transfers between devices, collect(): from_left = lax.ppermute(from_left, axis, ahead)  33.2 us
    reduce_scatter x1, waiting for transfers between devices, per_device(): lax.psum_scatter(key_grad_buf.reshape(1, buf_rows, feat_width).astype(jnp...  32.6 us
    dot_general x6, matrix products, head_step(): jnp.einsum('iqk,iqe->ike', dscore, query_head, preferred_element_type=jnp...  20.2 us
    dot_general x6, matrix products, head_step(): jnp.einsum('iqk,iqe->ike', weights_b, grad_head, preferred_element_type=j...  16 us
    dot_general x6, matrix products, head_step(): jnp.einsum('iqe,ike->iqk', grad_head, value_head, preferred_element_type=...  13.7 us
    reshape x1, local copies, waits for them, and re-layouts, attend(): value_sel_grad.reshape(tile_count, slot_count, tile_rows * feat_width)  13.3 us
  transfers between devices with their start and end apart: 7, of which 6 were waited for; matrix products, arithmetic and copies ran while one was open for 11% of the time, Pallas kernels for 0%

profile of v1, /device:TPU:0, one launch (start us, length us, event | category | flops | bytes accessed | tf_op | source)
XLA Modules:
  0.0 397.4 jit_solution(441169688991225653)
XLA Ops:
  8.7 3.1 collective-permute-start
  11.8 2.1 collective-permute-start.1
  15.4 17.2 %collective-permute-done = bf16[1,512,768]{2,1,0:T(8,128)(2,1)} collective-permute-done((bf16[1,512,768]{2,1,0:T(8,128)(2,1)}, bf16[1,512,768]{2,1,0:T(8,128)(2,1)}, u32[]{:S(2)}, u32[]{:S(2)}) %collective-permute-start) | collective-permute-done | bytes 786464 | tf_op jit(solution)/shard_map/ppermute | solution.py:19
  32.9 1.2 constant_dynamic-update-slice_fusion.3
  34.2 1.2 constant_dynamic-update-slice_fusion.2
  35.4 12.9 %collective-permute-done.1 = bf16[1,512,768]{2,1,0:T(8,128)(2,1)} collective-permute-done((bf16[1,512,768]{2,1,0:T(8,128)(2,1)}, bf16[1,512,768]{2,1,0:T(8,128)(2,1)}, u32[]{:S(2)}, u32[]{:S(2)}) %collective-permute-start.1) | collective-permute-done | bytes 786464 | tf_op jit(solution)/shard_map/ppermute | solution.py:24
  48.2 1.2 constant_dynamic-update-slice_fusion.1
  49.4 16.0 %collective-permute-done.2 = bf16[1,512,768]{2,1,0:T(8,128)(2,1)} collective-permute-done((bf16[1,512,768]{2,1,0:T(8,128)(2,1)}, bf16[1,512,768]{2,1,0:T(8,128)(2,1)}, u32[]{:S(2)}, u32[]{:S(2)}) %collective-permute-start.2) | collective-permute-done | bytes 786464 | tf_op jit(solution)/shard_map/ppermute | solution.py:19
  65.5 1.3 constant_dynamic-update-slice_fusion
  66.7 3.7 gather_fusion.1
  70.4 5.9 %fusion.28 = bf16[512,768]{1,0:T(8,128)(2,1)S(1)} fusion(bf16[768,3072]{1,0:T(8,128)(2,1)} %param.13, bf16[1,512,3072]{2,1,0:T(8,128)(2,1)} %all-gather.5.cloned.1.call-done), kind=kOutput, calls=%fused_computation.42 | convolution fusion | flops 2416312320 | bytes 8650752 | tf_op jit(solution)/shard_map/dot_general | solution.py:127
  76.3 45.9 %all-gather.3.cloned.1.call-done = bf16[1,2048,768]{2,1,0:T(8,128)(2,1)} async-done(((bf16[1,512,768]{2,1,0:T(8,128)(2,1)}), bf16[1,2048,768]{2,1,0:T(8,128)(2,1)}) %all-gather.3.cloned.1.call-update) | async-done | bytes 3145744 | tf_op jit(solution)/shard_map/all_gather | solution.py:136
  122.2 5.5 %gather_fusion = bf16[16,256,768]{2,1,0:T(8,128)(2,1)} fusion(bf16[8,256,768]{2,1,0:T(8,128)(2,1)} %bitcast.51, s32[1024]{0:T(1024)S(1)} %pad_clamp_fusion), kind=kCustom, calls=%fused_computation | custom fusion | bytes 12582976 | tf_op jit(solution)/shard_map/gather | solution.py:37
  127.8 5.4 %broadcast.108 = f32[2,2048,768]{2,1,0:T(8,128)} broadcast(f32[]{:T(128)} %constant.102.clone.1), dimensions={} | broadcast | bytes 12582916 | tf_op jit(solution)/shard_map/broadcast.13
  133.2 5.3 %broadcast.108.clone = f32[2,2048,768]{2,1,0:T(8,128)} broadcast(f32[]{:T(128)} %constant.102.clone.1), dimensions={} | broadcast | bytes 12582916 | tf_op jit(solution)/shard_map/broadcast.13
  138.6 92.5 %while.18 = (s32[]{:T(128)}, f32[2,256,768]{2,1,0:T(8,128)S(1)}, f32[2,2048,768]{2,1,0:T(8,128)}, f32[2,2048,768]{2,1,0:T(8,128)}, bf16[2,256,768]{2,1,0:T(8,128...) while((s32[]{:T(128)}, f32[2,256,768]{2,1,0:T(8,128)S(1)}, ...), condition=%wide.region_4.5_spmd.clone, body=%wide.region_0.4_spmd.clone.sunk | while | flops 1625164800 | bytes 36614328 | solution.py:86
  138.8 2.1 fusion.73
  141.7 2.6 convolution_dynamic-update-slice_fusion.2
  144.3 2.2 fusion.74
  146.5 2.3 multiply_convert_fusion.2
  148.7 3.4 fusion.76
  152.1 1.9 fusion.75
  154.2 2.1 fusion.73
  157.0 2.6 convolution_dynamic-update-slice_fusion.2
  159.7 2.2 fusion.74
  161.8 2.3 multiply_convert_fusion.2
  164.1 3.3 fusion.76
  167.5 1.9 fusion.75
  169.5 2.1 fusion.73
  172.3 2.7 convolution_dynamic-update-slice_fusion.2
  175.0 2.2 fusion.74
  177.2 2.3 multiply_convert_fusion.2
  179.5 3.3 fusion.76
  182.8 1.9 fusion.75
  184.9 2.1 fusion.73
  187.7 2.8 convolution_dynamic-update-slice_fusion.2
  190.4 2.2 fusion.74
  192.6 2.3 multiply_convert_fusion.2
  194.9 3.4 fusion.76
  198.3 1.9 fusion.75
  200.4 2.1 fusion.73
  203.2 2.7 convolution_dynamic-update-slice_fusion.2
  205.9 2.2 fusion.74
  208.1 2.3 multiply_convert_fusion.2
  210.3 3.4 fusion.76
  213.7 1.9 fusion.75
  215.8 2.1 fusion.73
  218.6 2.6 convolution_dynamic-update-slice_fusion.2
  221.3 2.2 fusion.74
  223.4 2.3 multiply_convert_fusion.2
  225.7 3.4 fusion.76
  229.1 1.9 fusion.75
  232.2 13.2 %reshape.176 = f32[2,8,196608]{2,1,0:T(8,128)} reshape(f32[2,2048,768]{2,1,0:T(8,128)} %get-tuple-element.161) | data formatting | bytes 25165824 | tf_op jit(solution)/shard_map/reshape | solution.py:96
  245.4 7.6 %fusion.24 = bf16[8,196608]{1,0:T(8,128)(2,1)S(1)} fusion(f32[2,8,196608]{2,1,0:T(8,128)} %reshape.176, s32[2,8]{1,0:T(2,128)S(1)} %fusion.41, pred[2,8]{1,0:T(4,128)(4,1)S(1)} %iota_compare_fusion.1), kind=kOutput, calls=%fused_computation.35 | convolution fusion | flops 303563008 | bytes 15728720 | tf_op jit(solution)/shard_map/imb,imr->br/dot_general | solution.py:93
  253.0 3.2 convert_element_type.94
  256.2 13.3 %reshape.177 = f32[2,8,196608]{2,1,0:T(8,128)} reshape(f32[2,2048,768]{2,1,0:T(8,128)} %get-tuple-element.162) | data formatting | bytes 25165824 | tf_op jit(solution)/shard_map/reshape | solution.py:102
  269.6 7.6 %fusion.25 = bf16[8,196608]{1,0:T(8,128)(2,1)S(1)} fusion(f32[2,8,196608]{2,1,0:T(8,128)} %reshape.177, s32[2,8]{1,0:T(2,128)S(1)} %fusion.41, pred[2,8]{1,0:T(4,128)(4,1)S(1)} %iota_compare_fusion.1), kind=kOutput, calls=%fused_computation.36 | convolution fusion | flops 303563008 | bytes 15728720 | tf_op jit(solution)/shard_map/imb,imr->br/dot_general | solution.py:99
  277.2 3.1 convert_element_type.96
  280.3 1.4 copy-done.3
  282.8 32.6 %reduce-scatter.3.cloned.1.call-done = bf16[1,512,768]{2,1,0:T(8,128)(2,1)} async-done(((bf16[1,2048,768]{2,1,0:T(8,128)(2,1)}), bf16[1,512,768]{2,1,0:T(8,128)(2,1)}) %reduce-scatter.3.cloned.1.call-update) | async-done | bytes 786448 | tf_op jit(solution)/shard_map/reduce_scatter | solution.py:146
  315.4 1.3 multiply_reduce_fusion.1
  316.8 61.6 %reduce-scatter.5.cloned.1.call-done = bf16[1,512,768]{2,1,0:T(8,128)(2,1)} async-done(((bf16[1,2048,768]{2,1,0:T(8,128)(2,1)}), bf16[1,512,768]{2,1,0:T(8,128)(2,1)}) %reduce-scatter.5.cloned.1.call-update) | async-done | bytes 786448 | tf_op jit(solution)/shard_map/reduce_scatter | solution.py:152
  378.5 1.3 multiply_reduce_fusion
  379.9 10.4 %psum.7 = f32[6,3]{0,1:T(4,128)S(1)} all-reduce(f32[6,3]{0,1:T(4,128)S(1)} %pad_maximum_fusion), channel_id=1, replica_groups=mesh['grp'=2,'seq'=4,'head'=2,'clip'=2] {'seq'}, use_global_device_ids=true, to_apply=%region_13.14 | all-reduce | flops 18 | bytes 144 | tf_op jit(solution)/shard_map/psum | solution.py:170
  (51 shorter events, 11.4 us)
Async XLA Ops:
  7.2 25.4 %copy-start = (s32[1,8]{1,0:T(1,128)S(1)}, s32[1,8]{1,0:T(1,128)}, u32[]{:S(2)}) copy-start(s32[1,8]{1,0:T(1,128)} %param.15) | copy-start | bytes 100
  7.2 63.2 %all-gather.5.cloned.1.call-start = ((), (), s32[]{:S(2)}) async-start(), calls=%async_computation.3 | async-start | bytes 4718592 | tf_op jit(solution)/shard_map/all_gather | solution.py:128
  7.9 114.3 %all-gather.3.cloned.1.call-start = ((), (), s32[]{:S(2)}) async-start(), calls=%async_computation.2 | async-start | bytes 3932160 | tf_op jit(solution)/shard_map/all_gather | solution.py:136
  8.7 306.7 %reduce-scatter.3.cloned.1.call-start = ((), (), s32[]{:S(2)}) async-start(), calls=%async_computation.4 | async-start | bytes 3932160 | tf_op jit(solution)/shard_map/reduce_scatter | solution.py:146
  8.7 23.9 %collective-permute-start = (bf16[1,512,768]{2,1,0:T(8,128)(2,1)}, bf16[1,512,768]{2,1,0:T(8,128)(2,1)}, u32[]{:S(2)}, u32[]{:S(2)}) collective-permute-start(bf16[1,512,768]{2,1,0:T(8,128)(2,1)} %param.11), channel_id=1, source_target_pairs={{0,4},{4,8},{8,12},{12,0},{1,5},{5,9},{9,13},{13,1},{2,6},{6,10},{... | collective-permute-start | bytes 2359304 | tf_op jit(solution)/shard_map/ppermute | solution.py:19
  11.8 36.4 %collective-permute-start.1 = (bf16[1,512,768]{2,1,0:T(8,128)(2,1)}, bf16[1,512,768]{2,1,0:T(8,128)(2,1)}, u32[]{:S(2)}, u32[]{:S(2)}) collective-permute-start(bf16[1,512,768]{2,1,0:T(8,128)(2,1)} %param.11), channel_id=1, source_target_pairs={{0,12},{4,0},{8,4},{12,8},{1,13},{5,1},{9,5},{13,9},{2,14},{6,2},{... | collective-permute-start | bytes 2359304 | tf_op jit(solution)/shard_map/ppermute | solution.py:24
  32.6 32.9 %collective-permute-start.2 = (bf16[1,512,768]{2,1,0:T(8,128)(2,1)}, bf16[1,512,768]{2,1,0:T(8,128)(2,1)}, u32[]{:S(2)}, u32[]{:S(2)}) collective-permute-start(bf16[1,512,768]{2,1,0:T(8,128)(2,1)} %collective-permute-done), channel_id=1, source_target_pairs={{0,4},{4,8},{8,12},{12,0},{1,5},{5,9},{9,13},{13,1},{2,6},{6,10},{... | collective-permute-start | bytes 2359304 | tf_op jit(solution)/shard_map/ppermute | solution.py:19
  231.0 1.1 copy-start.2
  256.2 122.3 %reduce-scatter.5.cloned.1.call-start = ((), (), s32[]{:S(2)}) async-start(), calls=%async_computation.5 | async-start | bytes 3932160 | tf_op jit(solution)/shard_map/reduce_scatter | solution.py:152
  277.2 113.7 %copy-start.1 = (s32[1,8]{1,0:T(1,128)S(1)}, s32[1,8]{1,0:T(1,128)}, u32[]{:S(2)}) copy-start(s32[1,8]{1,0:T(1,128)} %param.15) | copy-start | bytes 100
  280.3 1.4 copy-start.3
Sparse Core Ops, SparseCore 0:
  9.5 47.6 all-gather.4
  58.8 63.4 all-gather.2
  256.3 59.0 reduce-scatter.2
  318.1 60.2 reduce-scatter.4
